TPU v7x, 32 devices: a whole 2x2x4 slice. The times are simulated.
32 devices in a mesh: row: 8 (over z, core), col: 4 (over y, x).
Axes of the slice: x: 2, y: 2, z: 4, core: 2. Of those that a mesh axis runs over, the one named last changes fastest.
Arguments:
- points: bfloat16 [2048, 1024], P(('row', 'col')), may hold values from -6 to 6
- factor: float32 [2048, 256], P(('row', 'col')), may hold values from 0 to 1
Outputs:
- factor_out: float32 [2048, 256], P(('row', 'col'))
All inputs are finite; a program needn't handle non-finite values.
Results may differ from a plain program's by a relative error of at most 0.002.
The roundings to bfloat16 on the way count: a program that leaves them out, or rounds other values in their place, can miss the bound.
Values may be sent and summed in bfloat16 or wider, within the bound.
A program may use at most 64 MiB of HBM per device.

v0:
```python
import math
import jax
import jax.numpy as jnp
from jax import lax
from jax.sharding import PartitionSpec as P

EMBED_WIDTH = 1024
ITERS = 2


def shards(points, factor):
    nrow = lax.axis_size("row")
    ncol = lax.axis_size("col")
    pts = points.shape[0]
    rank = factor.shape[1]
    total = pts * nrow * ncol
    row_pts = lax.all_gather(points, "col", axis=0, tiled=True)
    col_pts = lax.all_gather(points, "row", axis=0, tiled=True)
    gram_matrix = lax.dot_general(
        row_pts, col_pts, (((1,), (1,)), ((), ())), preferred_element_type=jnp.float32
    )
    row_sq = jnp.sum(jnp.square(row_pts.astype(jnp.float32)), axis=1)
    col_sq = jnp.sum(jnp.square(col_pts.astype(jnp.float32)), axis=1)
    kern = jnp.exp((2.0 * gram_matrix - row_sq[:, None] - col_sq[None, :]) * (0.5 / EMBED_WIDTH))
    row_sum, band = lax.psum((jnp.sum(kern, axis=1), jnp.sum(kern)), "col")
    col_sum, grand = lax.psum((jnp.sum(kern, axis=0), band), "row")
    affinity = (
        kern - row_sum[:, None] / total - col_sum[None, :] / total + grand / (total * total)
    ).astype(jnp.bfloat16)
    unit = 2.0 / math.sqrt(total * rank)
    h = factor * unit
    for step in range(ITERS):
        hb = h.astype(jnp.bfloat16)
        copies = lax.all_gather(hb, "row", axis=0, tiled=True)
        ah = lax.psum_scatter(
            jnp.dot(affinity, copies, preferred_element_type=jnp.float32),
            "col",
            scatter_dimension=0,
            tiled=True,
        )
        local_gram = lax.dot_general(
            h, h, (((0,), (0,)), ((), ())), precision=lax.Precision.HIGHEST
        )
        hh = lax.psum(local_gram, ("row", "col"))
        scale = 0.5 / jnp.sqrt(jnp.sum(hh * hh) + 1e-06)
        h = jnp.maximum(h - scale * (jnp.dot(h, hh, precision=lax.Precision.HIGHEST) - ah), 0.0)
    return h / unit


def solution(mesh):
    in_specs = (P(("row", "col"), None), P(("row", "col"), None))
    out_specs = P(("row", "col"), None)
    return jax.shard_map(shards, mesh=mesh, in_specs=in_specs, out_specs=out_specs, check_vma=False)
```

profile of v0, /device:TPU:0, one launch (start us, length us, event | category | flops | bytes accessed | tf_op | source)
XLA Modules:
  0.0 301.0 jit_solution(7194826416192646812)
XLA Ops:
  7.4 0.7 all-gather.2.cloned.1.call-update
  8.1 0.0 all-reduce.5.cloned.1.call-start
  8.1 2.0 fusion.12
  10.2 0.0 reduce-scatter.3.cloned.1.call-start
  10.3 11.9 %all_gather.12 = bf16[256,1024]{1,0:T(8,128)(2,1)S(1)} all-gather(bf16[64,1024]{1,0:T(8,128)(2,1)} %param.2), channel_id=1, replica_groups=mesh['row'=8,'col'=4] {'col'}, dimensions={0}, use_global_device_ids=true | all-gather | bytes 655360 | tf_op jit(solution)/shard_map/all_gather | solution.py:17
  22.2 0.2 multiply_reduce_fusion.1
  22.3 15.2 %all_gather.14 = bf16[512,256]{1,0:T(8,128)(2,1)S(1)} all-gather(bf16[64,256]{1,0:T(8,128)(2,1)S(1)} %multiply_convert_fusion), channel_id=1, replica_groups=mesh['row'=8,'col'=4] {'row'}, dimensions={0}, use_global_device_ids=true | all-gather | bytes 294912 | tf_op jit(solution)/shard_map/all_gather | solution.py:34
  37.6 1.6 multiply_reduce_fusion
  39.2 1.2 fusion.20
  40.4 9.6 %all-reduce.1 = (f32[]{:T(128)}, f32[256]{0:T(256)S(1)}) all-reduce(f32[]{:T(128)} %get-tuple-element.6, f32[256]{0:T(256)S(1)} %get-tuple-element.5), channel_id=1, replica_groups=mesh['row'=8,'col'=4] {'col'}, use_global_device_ids=true, to_apply=%region_9.0 | all-reduce | flops 257 | bytes 2056 | tf_op jit(solution)/shard_map/psum | solution.py:25
  50.0 15.4 %all-reduce = (f32[]{:T(128)}, f32[512]{0:T(512)S(1)}) all-reduce(f32[]{:T(128)} %get-tuple-element.10, f32[512]{0:T(512)S(1)} %get-tuple-element.7), channel_id=1, replica_groups=mesh['row'=8,'col'=4] {'row'}, use_global_device_ids=true, to_apply=%region_10.0 | all-reduce | flops 513 | bytes 4104 | tf_op jit(solution)/shard_map/psum | solution.py:26
  66.1 1.0 fusion.19
  67.1 0.0 all-reduce.7.cloned.1.call-start
  67.2 78.5 %all-reduce.5.cloned.1.call-done = f32[256,256]{1,0:T(8,128)} async-done(((f32[256,256]{1,0:T(8,128)}), f32[256,256]{1,0:T(8,128)}) %all-reduce.5.cloned.1.call-update) | async-done | bytes 262160 | tf_op jit(solution)/shard_map/psum | solution.py:44
  145.6 1.6 multiply_reduce_fusion.3
  147.9 0.0 reduce-scatter.3.cloned.1.call-done
  148.0 1.2 fusion.21
  149.2 14.2 %all_gather.15 = bf16[512,256]{1,0:T(8,128)(2,1)S(1)} all-gather(bf16[64,256]{1,0:T(8,128)(2,1)S(1)} %get-tuple-element.13), channel_id=1, replica_groups=mesh['row'=8,'col'=4] {'row'}, dimensions={0}, use_global_device_ids=true | all-gather | bytes 294912 | tf_op jit(solution)/shard_map/all_gather | solution.py:34
  163.4 1.1 fusion.22
  164.5 0.0 reduce-scatter.5.cloned.1.call-start
  164.6 1.0 fusion.18
  165.6 124.1 %all-reduce.7.cloned.1.call-done = f32[256,256]{1,0:T(8,128)} async-done(((f32[256,256]{1,0:T(8,128)}), f32[256,256]{1,0:T(8,128)}) %all-reduce.7.cloned.1.call-update) | async-done | bytes 262160 | tf_op jit(solution)/shard_map/psum | solution.py:44
  289.7 1.6 multiply_reduce_fusion.2
  292.0 1.8 fusion.7
  (14 shorter events, 0.1 us)
Async XLA Ops:
  7.4 14.8 %copy-start.1 = (f32[64,256]{1,0:T(8,128)S(1)}, f32[64,256]{1,0:T(8,128)}, u32[]{:S(2)}) copy-start(f32[64,256]{1,0:T(8,128)} %param.3) | copy-start | bytes 196612
  7.4 30.2 %all-gather.2.cloned.1.call-start = ((), (), s32[]{:S(2)}) async-start(), calls=%async_computation.3 | async-start | bytes 1179648 | tf_op jit(solution)/shard_map/all_gather | solution.py:18
  8.1 137.5 %all-reduce.5.cloned.1.call-start = ((), (), s32[]{:S(2)}) async-start(), calls=%async_computation.2 | async-start | bytes 524288 | tf_op jit(solution)/shard_map/psum | solution.py:44
  10.2 137.8 %reduce-scatter.3.cloned.1.call-start = ((), (), s32[]{:S(2)}) async-start(), calls=%async_computation.4 | async-start | bytes 327680 | tf_op jit(solution)/shard_map/reduce_scatter | solution.py:35
  37.6 1.6 copy-start
  67.1 222.6 %all-reduce.7.cloned.1.call-start = ((), (), s32[]{:S(2)}) async-start(), calls=%async_computation.5 | async-start | bytes 524288 | tf_op jit(solution)/shard_map/psum | solution.py:44
  164.5 127.5 %reduce-scatter.5.cloned.1.call-start = ((), (), s32[]{:S(2)}) async-start(), calls=%async_computation.6 | async-start | bytes 327680 | tf_op jit(solution)/shard_map/reduce_scatter | solution.py:35
Sparse Core Ops, SparseCore 0:
  9.8 26.2 all-gather.1
  67.2 21.1 reduce-scatter.2
  168.1 23.4 reduce-scatter.4
Sparse Core Ops, SparseCore 1:
  14.1 131.5 all-reduce.4
  164.6 125.0 all-reduce.6
where the time goes:
time: 301 us
  waiting for transfers between devices  203 us (67%)
  blocking collectives  66.4 us (22%)
  between operations  16.6 us (6%)
  matrix products  9.4 us (3%)
  other arithmetic  5.03 us (2%)
    psum x2, waiting for transfers between devices, shards(): hh = lax.psum(local_gram, ('row', 'col'))  203 us
    all_gather x2, blocking collectives, shards(): copies = lax.all_gather(hb, 'row', axis=0, tiled=True)  29.4 us
    psum x1, blocking collectives, shards(): col_sum, grand = lax.psum((jnp.sum(kern, axis=0), band), 'row')  15.4 us
    all_gather x1, blocking collectives, shards(): row_pts = lax.all_gather(points, 'col', axis=0, tiled=True)  11.9 us
    psum x1, blocking collectives, shards(): row_sum, band = lax.psum((jnp.sum(kern, axis=1), jnp.sum(kern)), 'col')  9.6 us
  transfers between devices with their start and end apart: 5, of which 2 were waited for; matrix products, arithmetic and copies ran while one was open for 3% of the time, Pallas kernels for 0%

commit v1 on v0

--- a/solution.py
+++ b/solution.py
@@ -31,7 +31,14 @@
     h = factor * unit
     for step in range(ITERS):
         hb = h.astype(jnp.bfloat16)
-        copies = lax.all_gather(hb, "row", axis=0, tiled=True)
+        ring = [hb]
+        for hop in range(7):
+            ring.append(lax.ppermute(ring[-1], "row", [(dev, (dev + 1) % 8) for dev in range(8)]))
+        copies = jnp.roll(
+            jnp.concatenate(ring[::-1], axis=0),
+            (lax.axis_index("row") + 1) * ring[0].shape[0],
+            axis=0,
+        )
         ah = lax.psum_scatter(
             jnp.dot(affinity, copies, preferred_element_type=jnp.float32),
             "col",

time: 301 us -> 336 us (1.12)
  waiting for transfers between devices: 203 us -> 267 us
  blocking collectives: 66.4 us -> 34.8 us
    ppermute x0 -> x14, waiting for transfers between devices: none -> 64.8 us  [shards(): lax.ppermute(ring[-1], 'row', [(dev, (dev + 1) % 8) for dev in range(8)])]
    all_gather x2 -> x0, blocking collectives: 29.4 us -> none  [shards(): copies = lax.all_gather(hb, 'row', axis=0, tiled=True)]
  transfers between devices with their start and end apart: 5 -> 19, of which waited for: 2 -> 15; matrix products, arithmetic and copies ran while one was open for 3% -> 4% of each run, Pallas kernels for 0% -> 0%
where the time goes in v1:
time: 336 us
  waiting for transfers between devices  267 us (79%)
  blocking collectives  34.8 us (10%)
  between operations  16.8 us (5%)
  matrix products  10.2 us (3%)
  other arithmetic  5.88 us (2%)
    psum x2, waiting for transfers between devices, shards(): hh = lax.psum(local_gram, ('row', 'col'))  202 us
    ppermute x14, waiting for transfers between devices, shards(): lax.ppermute(ring[-1], 'row', [(dev, (dev + 1) % 8) for dev in range(8)])  64.8 us
    psum x1, blocking collectives, shards(): col_sum, grand = lax.psum((jnp.sum(kern, axis=0), band), 'row')  14.2 us
    all_gather x1, blocking collectives, shards(): row_pts = lax.all_gather(points, 'col', axis=0, tiled=True)  11.1 us
    psum x1, blocking collectives, shards(): row_sum, band = lax.psum((jnp.sum(kern, axis=1), jnp.sum(kern)), 'col')  9.53 us
  transfers between devices with their start and end apart: 19, of which 15 were waited for; matrix products, arithmetic and copies ran while one was open for 4% of the time, Pallas kernels for 0%

profile of v1, /device:TPU:0, one launch (start us, length us, event | category | flops | bytes accessed | tf_op | source)
XLA Modules:
  0.0 335.8 jit_solution(8179274356328408126)
XLA Ops:
  9.5 5.6 %collective-permute-done = bf16[64,256]{1,0:T(8,128)(2,1)S(1)} collective-permute-done((bf16[64,256]{1,0:T(8,128)(2,1)S(1)}, bf16[64,256]{1,0:T(8,128)(2,1)S(1)}, u32[]{:S(2)}, u32[]{:S(2)}) %collective-permute-start) | collective-permute-done | bytes 32800 | tf_op jit(solution)/shard_map/ppermute | solution.py:36
  15.1 5.1 %collective-permute-done.1 = bf16[64,256]{1,0:T(8,128)(2,1)S(1)} collective-permute-done((bf16[64,256]{1,0:T(8,128)(2,1)S(1)}, bf16[64,256]{1,0:T(8,128)(2,1)S(1)}, u32[]{:S(2)}, u32[]{:S(2)}) %collective-permute-start.1) | collective-permute-done | bytes 32800 | tf_op jit(solution)/shard_map/ppermute | solution.py:36
  20.2 5.6 %collective-permute-done.2 = bf16[64,256]{1,0:T(8,128)(2,1)S(1)} collective-permute-done((bf16[64,256]{1,0:T(8,128)(2,1)S(1)}, bf16[64,256]{1,0:T(8,128)(2,1)S(1)}, u32[]{:S(2)}, u32[]{:S(2)}) %collective-permute-start.2) | collective-permute-done | bytes 32800 | tf_op jit(solution)/shard_map/ppermute | solution.py:36
  25.8 5.8 %collective-permute-done.3 = bf16[64,256]{1,0:T(8,128)(2,1)S(1)} collective-permute-done((bf16[64,256]{1,0:T(8,128)(2,1)S(1)}, bf16[64,256]{1,0:T(8,128)(2,1)S(1)}, u32[]{:S(2)}, u32[]{:S(2)}) %collective-permute-start.3) | collective-permute-done | bytes 32800 | tf_op jit(solution)/shard_map/ppermute | solution.py:36
  31.6 2.0 fusion.18
  33.7 3.0 collective-permute-done.4
  36.8 11.1 %all_gather.6 = bf16[256,1024]{1,0:T(8,128)(2,1)S(1)} all-gather(bf16[64,1024]{1,0:T(8,128)(2,1)} %param.4), channel_id=1, replica_groups=mesh['row'=8,'col'=4] {'col'}, dimensions={0}, use_global_device_ids=true | all-gather | bytes 655360 | tf_op jit(solution)/shard_map/all_gather | solution.py:17
  48.1 5.0 %collective-permute-done.6 = bf16[64,256]{1,0:T(8,128)(2,1)S(1)} collective-permute-done((bf16[64,256]{1,0:T(8,128)(2,1)S(1)}, bf16[64,256]{1,0:T(8,128)(2,1)S(1)}, u32[]{:S(2)}, u32[]{:S(2)}) %collective-permute-start.6) | collective-permute-done | bytes 32800 | tf_op jit(solution)/shard_map/ppermute | solution.py:36
  53.2 1.6 multiply_reduce_fusion
  56.0 9.5 %all-reduce.1 = (f32[]{:T(128)}, f32[256]{0:T(256)S(1)}) all-reduce(f32[]{:T(128)} %get-tuple-element.7, f32[256]{0:T(256)S(1)} %get-tuple-element.6), channel_id=1, replica_groups=mesh['row'=8,'col'=4] {'col'}, use_global_device_ids=true, to_apply=%region_9.10 | all-reduce | flops 257 | bytes 2056 | tf_op jit(solution)/shard_map/psum | solution.py:25
  65.6 14.2 %all-reduce = (f32[]{:T(128)}, f32[512]{0:T(512)S(1)}) all-reduce(f32[]{:T(128)} %get-tuple-element.11, f32[512]{0:T(512)S(1)} %get-tuple-element.8), channel_id=1, replica_groups=mesh['row'=8,'col'=4] {'row'}, use_global_device_ids=true, to_apply=%region_10.11 | all-reduce | flops 513 | bytes 4104 | tf_op jit(solution)/shard_map/psum | solution.py:26
  81.9 79.8 %all-reduce.5.cloned.1.call-done = f32[256,256]{1,0:T(8,128)} async-done(((f32[256,256]{1,0:T(8,128)}), f32[256,256]{1,0:T(8,128)}) %all-reduce.5.cloned.1.call-update) | async-done | bytes 262160 | tf_op jit(solution)/shard_map/psum | solution.py:51
  161.7 1.6 multiply_reduce_fusion.3
  165.3 5.1 %collective-permute-done.7 = bf16[64,256]{1,0:T(8,128)(2,1)S(1)} collective-permute-done((bf16[64,256]{1,0:T(8,128)(2,1)S(1)}, bf16[64,256]{1,0:T(8,128)(2,1)S(1)}, u32[]{:S(2)}, u32[]{:S(2)}) %collective-permute-start.7) | collective-permute-done | bytes 32800 | tf_op jit(solution)/shard_map/ppermute | solution.py:36
  170.4 5.1 %collective-permute-done.8 = bf16[64,256]{1,0:T(8,128)(2,1)S(1)} collective-permute-done((bf16[64,256]{1,0:T(8,128)(2,1)S(1)}, bf16[64,256]{1,0:T(8,128)(2,1)S(1)}, u32[]{:S(2)}, u32[]{:S(2)}) %collective-permute-start.8) | collective-permute-done | bytes 32800 | tf_op jit(solution)/shard_map/ppermute | solution.py:36
  175.6 5.1 %collective-permute-done.9 = bf16[64,256]{1,0:T(8,128)(2,1)S(1)} collective-permute-done((bf16[64,256]{1,0:T(8,128)(2,1)S(1)}, bf16[64,256]{1,0:T(8,128)(2,1)S(1)}, u32[]{:S(2)}, u32[]{:S(2)}) %collective-permute-start.9) | collective-permute-done | bytes 32800 | tf_op jit(solution)/shard_map/ppermute | solution.py:36
  180.7 5.1 %collective-permute-done.10 = bf16[64,256]{1,0:T(8,128)(2,1)S(1)} collective-permute-done((bf16[64,256]{1,0:T(8,128)(2,1)S(1)}, bf16[64,256]{1,0:T(8,128)(2,1)S(1)}, u32[]{:S(2)}, u32[]{:S(2)}) %collective-permute-start.10) | collective-permute-done | bytes 32800 | tf_op jit(solution)/shard_map/ppermute | solution.py:36
  185.9 5.1 %collective-permute-done.11 = bf16[64,256]{1,0:T(8,128)(2,1)S(1)} collective-permute-done((bf16[64,256]{1,0:T(8,128)(2,1)S(1)}, bf16[64,256]{1,0:T(8,128)(2,1)S(1)}, u32[]{:S(2)}, u32[]{:S(2)}) %collective-permute-start.11) | collective-permute-done | bytes 32800 | tf_op jit(solution)/shard_map/ppermute | solution.py:36
  191.0 5.1 %collective-permute-done.12 = bf16[64,256]{1,0:T(8,128)(2,1)S(1)} collective-permute-done((bf16[64,256]{1,0:T(8,128)(2,1)S(1)}, bf16[64,256]{1,0:T(8,128)(2,1)S(1)}, u32[]{:S(2)}, u32[]{:S(2)}) %collective-permute-start.12) | collective-permute-done | bytes 32800 | tf_op jit(solution)/shard_map/ppermute | solution.py:36
  197.3 3.9 %collective-permute-done.13 = bf16[64,256]{1,0:T(8,128)(2,1)S(1)} collective-permute-done((bf16[64,256]{1,0:T(8,128)(2,1)S(1)}, bf16[64,256]{1,0:T(8,128)(2,1)S(1)}, u32[]{:S(2)}, u32[]{:S(2)}) %collective-permute-start.13) | collective-permute-done | bytes 32800 | tf_op jit(solution)/shard_map/ppermute | solution.py:36
  201.3 1.4 fusion.12
  202.7 121.7 %all-reduce.7.cloned.1.call-done = f32[256,256]{1,0:T(8,128)} async-done(((f32[256,256]{1,0:T(8,128)}), f32[256,256]{1,0:T(8,128)}) %all-reduce.7.cloned.1.call-update) | async-done | bytes 262160 | tf_op jit(solution)/shard_map/psum | solution.py:51
  324.5 1.6 multiply_reduce_fusion.2
  326.8 1.8 fusion.7
  (56 shorter events, 7.7 us)
Async XLA Ops:
  7.4 45.8 %all-gather.2.cloned.1.call-start = ((), (), s32[]{:S(2)}) async-start(), calls=%async_computation.3 | async-start | bytes 1179648 | tf_op jit(solution)/shard_map/all_gather | solution.py:18
  8.1 153.6 %all-reduce.5.cloned.1.call-start = ((), (), s32[]{:S(2)}) async-start(), calls=%async_computation.2 | async-start | bytes 524288 | tf_op jit(solution)/shard_map/psum | solution.py:51
  9.0 6.1 %collective-permute-start = (bf16[64,256]{1,0:T(8,128)(2,1)S(1)}, bf16[64,256]{1,0:T(8,128)(2,1)S(1)}, u32[]{:S(2)}, u32[]{:S(2)}) collective-permute-start(bf16[64,256]{1,0:T(8,128)(2,1)S(1)} %multiply_convert_fusion), channel_id=1, source_target_pairs={{0,4},{4,8},{8,12},{12,16},{16,20},{20,24},{24,28},{28,0},{1,5},{5... | collective-permute-start | bytes 98312 | tf_op jit(solution)/shard_map/ppermute | solution.py:36
  15.1 5.1 %collective-permute-start.1 = (bf16[64,256]{1,0:T(8,128)(2,1)S(1)}, bf16[64,256]{1,0:T(8,128)(2,1)S(1)}, u32[]{:S(2)}, u32[]{:S(2)}) collective-permute-start(bf16[64,256]{1,0:T(8,128)(2,1)S(1)} %collective-permute-done), channel_id=1, source_target_pairs={{0,4},{4,8},{8,12},{12,16},{16,20},{20,24},{24,28},{28,0},{1,5},{5... | collective-permute-start | bytes 98312 | tf_op jit(solution)/shard_map/ppermute | solution.py:36
  20.2 5.6 %collective-permute-start.2 = (bf16[64,256]{1,0:T(8,128)(2,1)S(1)}, bf16[64,256]{1,0:T(8,128)(2,1)S(1)}, u32[]{:S(2)}, u32[]{:S(2)}) collective-permute-start(bf16[64,256]{1,0:T(8,128)(2,1)S(1)} %collective-permute-done.1), channel_id=1, source_target_pairs={{0,4},{4,8},{8,12},{12,16},{16,20},{20,24},{24,28},{28,0},{1,5},{5... | collective-permute-start | bytes 98312 | tf_op jit(solution)/shard_map/ppermute | solution.py:36
  25.8 5.8 %collective-permute-start.3 = (bf16[64,256]{1,0:T(8,128)(2,1)S(1)}, bf16[64,256]{1,0:T(8,128)(2,1)S(1)}, u32[]{:S(2)}, u32[]{:S(2)}) collective-permute-start(bf16[64,256]{1,0:T(8,128)(2,1)S(1)} %collective-permute-done.2), channel_id=1, source_target_pairs={{0,4},{4,8},{8,12},{12,16},{16,20},{20,24},{24,28},{28,0},{1,5},{5... | collective-permute-start | bytes 98312 | tf_op jit(solution)/shard_map/ppermute | solution.py:36
  31.6 5.1 %collective-permute-start.4 = (bf16[64,256]{1,0:T(8,128)(2,1)S(1)}, bf16[64,256]{1,0:T(8,128)(2,1)S(1)}, u32[]{:S(2)}, u32[]{:S(2)}) collective-permute-start(bf16[64,256]{1,0:T(8,128)(2,1)S(1)} %collective-permute-done.3), channel_id=1, source_target_pairs={{0,4},{4,8},{8,12},{12,16},{16,20},{20,24},{24,28},{28,0},{1,5},{5... | collective-permute-start | bytes 98312 | tf_op jit(solution)/shard_map/ppermute | solution.py:36
  33.7 19.5 %copy-start = (f32[64,256]{1,0:T(8,128)S(1)}, f32[64,256]{1,0:T(8,128)}, u32[]{:S(2)}) copy-start(f32[64,256]{1,0:T(8,128)} %param.5) | copy-start | bytes 196612
  33.7 130.3 %reduce-scatter.3.cloned.1.call-start = ((), (), s32[]{:S(2)}) async-start(), calls=%async_computation.4 | async-start | bytes 327680 | tf_op jit(solution)/shard_map/reduce_scatter | solution.py:42
  36.8 11.1 %collective-permute-start.5 = (bf16[64,256]{1,0:T(8,128)(2,1)S(1)}, bf16[64,256]{1,0:T(8,128)(2,1)S(1)}, u32[]{:S(2)}, u32[]{:S(2)}) collective-permute-start(bf16[64,256]{1,0:T(8,128)(2,1)S(1)} %collective-permute-done.4), channel_id=1, source_target_pairs={{0,4},{4,8},{8,12},{12,16},{16,20},{20,24},{24,28},{28,0},{1,5},{5... | collective-permute-start | bytes 98312 | tf_op jit(solution)/shard_map/ppermute | solution.py:36
  47.8 5.2 %collective-permute-start.6 = (bf16[64,256]{1,0:T(8,128)(2,1)S(1)}, bf16[64,256]{1,0:T(8,128)(2,1)S(1)}, u32[]{:S(2)}, u32[]{:S(2)}) collective-permute-start(bf16[64,256]{1,0:T(8,128)(2,1)S(1)} %collective-permute-done.5), channel_id=1, source_target_pairs={{0,4},{4,8},{8,12},{12,16},{16,20},{20,24},{24,28},{28,0},{1,5},{5... | collective-permute-start | bytes 98312 | tf_op jit(solution)/shard_map/ppermute | solution.py:36
  53.2 1.6 copy-start.1
  81.8 242.7 %all-reduce.7.cloned.1.call-start = ((), (), s32[]{:S(2)}) async-start(), calls=%async_computation.5 | async-start | bytes 524288 | tf_op jit(solution)/shard_map/psum | solution.py:51
  165.2 5.2 %collective-permute-start.7 = (bf16[64,256]{1,0:T(8,128)(2,1)S(1)}, bf16[64,256]{1,0:T(8,128)(2,1)S(1)}, u32[]{:S(2)}, u32[]{:S(2)}) collective-permute-start(bf16[64,256]{1,0:T(8,128)(2,1)S(1)} %get-tuple-element.14), channel_id=1, source_target_pairs={{0,4},{4,8},{8,12},{12,16},{16,20},{20,24},{24,28},{28,0},{1,5},{5... | collective-permute-start | bytes 98312 | tf_op jit(solution)/shard_map/ppermute | solution.py:36
  170.4 5.1 %collective-permute-start.8 = (bf16[64,256]{1,0:T(8,128)(2,1)S(1)}, bf16[64,256]{1,0:T(8,128)(2,1)S(1)}, u32[]{:S(2)}, u32[]{:S(2)}) collective-permute-start(bf16[64,256]{1,0:T(8,128)(2,1)S(1)} %collective-permute-done.7), channel_id=1, source_target_pairs={{0,4},{4,8},{8,12},{12,16},{16,20},{20,24},{24,28},{28,0},{1,5},{5... | collective-permute-start | bytes 98312 | tf_op jit(solution)/shard_map/ppermute | solution.py:36
  175.6 5.1 %collective-permute-start.9 = (bf16[64,256]{1,0:T(8,128)(2,1)S(1)}, bf16[64,256]{1,0:T(8,128)(2,1)S(1)}, u32[]{:S(2)}, u32[]{:S(2)}) collective-permute-start(bf16[64,256]{1,0:T(8,128)(2,1)S(1)} %collective-permute-done.8), channel_id=1, source_target_pairs={{0,4},{4,8},{8,12},{12,16},{16,20},{20,24},{24,28},{28,0},{1,5},{5... | collective-permute-start | bytes 98312 | tf_op jit(solution)/shard_map/ppermute | solution.py:36
  180.7 5.1 %collective-permute-start.10 = (bf16[64,256]{1,0:T(8,128)(2,1)S(1)}, bf16[64,256]{1,0:T(8,128)(2,1)S(1)}, u32[]{:S(2)}, u32[]{:S(2)}) collective-permute-start(bf16[64,256]{1,0:T(8,128)(2,1)S(1)} %collective-permute-done.9), channel_id=1, source_target_pairs={{0,4},{4,8},{8,12},{12,16},{16,20},{20,24},{24,28},{28,0},{1,5},{5... | collective-permute-start | bytes 98312 | tf_op jit(solution)/shard_map/ppermute | solution.py:36
  185.9 5.1 %collective-permute-start.11 = (bf16[64,256]{1,0:T(8,128)(2,1)S(1)}, bf16[64,256]{1,0:T(8,128)(2,1)S(1)}, u32[]{:S(2)}, u32[]{:S(2)}) collective-permute-start(bf16[64,256]{1,0:T(8,128)(2,1)S(1)} %collective-permute-done.10), channel_id=1, source_target_pairs={{0,4},{4,8},{8,12},{12,16},{16,20},{20,24},{24,28},{28,0},{1,5},{5... | collective-permute-start | bytes 98312 | tf_op jit(solution)/shard_map/ppermute | solution.py:36
  191.0 5.1 %collective-permute-start.12 = (bf16[64,256]{1,0:T(8,128)(2,1)S(1)}, bf16[64,256]{1,0:T(8,128)(2,1)S(1)}, u32[]{:S(2)}, u32[]{:S(2)}) collective-permute-start(bf16[64,256]{1,0:T(8,128)(2,1)S(1)} %collective-permute-done.11), channel_id=1, source_target_pairs={{0,4},{4,8},{8,12},{12,16},{16,20},{20,24},{24,28},{28,0},{1,5},{5... | collective-permute-start | bytes 98312 | tf_op jit(solution)/shard_map/ppermute | solution.py:36
  196.1 5.1 %collective-permute-start.13 = (bf16[64,256]{1,0:T(8,128)(2,1)S(1)}, bf16[64,256]{1,0:T(8,128)(2,1)S(1)}, u32[]{:S(2)}, u32[]{:S(2)}) collective-permute-start(bf16[64,256]{1,0:T(8,128)(2,1)S(1)} %collective-permute-done.12), channel_id=1, source_target_pairs={{0,4},{4,8},{8,12},{12,16},{16,20},{20,24},{24,28},{28,0},{1,5},{5... | collective-permute-start | bytes 98312 | tf_op jit(solution)/shard_map/ppermute | solution.py:36
  197.3 129.5 %reduce-scatter.5.cloned.1.call-start = ((), (), s32[]{:S(2)}) async-start(), calls=%async_computation.6 | async-start | bytes 327680 | tf_op jit(solution)/shard_map/reduce_scatter | solution.py:42
Sparse Core Ops, SparseCore 0:
  9.8 24.9 all-gather.1
  81.9 21.3 reduce-scatter.2
  202.9 23.4 reduce-scatter.4
Sparse Core Ops, SparseCore 1:
  33.8 127.9 all-reduce.4
  197.4 127.1 all-reduce.6
